TPU v7x, 256 devices: a whole 4x4x8 slice. The times are simulated.
256 devices in a mesh: rep: 8 (over z), exp: 32 (over x, y, core).
Axes of the slice: x: 4, y: 4, z: 8, core: 2. Of those that a mesh axis runs over, the one named last changes fastest.
Arguments:
- tokens: bfloat16 [4096, 4096], P(('rep', 'exp')), may hold values from -6 to 6
- routed_experts: int32 [4096, 8], P(('rep', 'exp')), may hold values from 0 to 63, all different within a row; in each aligned block of 16 rows (0 to 15, 16 to 31, ...) at most 3 rows name the same one
- route_weights: float32 [4096, 8], P(('rep', 'exp')), may hold values from 0.02 to 0.5
- gate_weight: bfloat16 [64, 1536, 4096], P('exp', 'rep'), may hold values from -0.09375 to 0.09375
- up_weight: bfloat16 [64, 1536, 4096], P('exp', 'rep'), may hold values from -0.09375 to 0.09375
- down_weight: bfloat16 [64, 1536, 4096], P('exp', 'rep'), may hold values from -0.15625 to 0.15625
Outputs:
- layer_output: bfloat16 [4096, 4096], P(('rep', 'exp'))
Inputs may be any that keep to these rules, and one draw needn't show every extreme that they name: `routed_experts`: each token names 8 different experts. Among the 16 tokens of one device (aligned blocks of rows), no expert is named more than 3 times, a bound that some block reaches.
All inputs are finite; a program needn't handle non-finite values.
Results may differ from a plain program's by a relative error of at most 0.01.
Values may be sent and summed in bfloat16 or wider, within the bound.
A program may use at most 128 MiB of HBM per device.

v0:
```python
import jax
import jax.numpy as jnp
from jax import lax
from jax.sharding import PartitionSpec as P


def slot_table(experts, expert_count, capacity):
    blocks = experts.shape[0]
    flattened = experts.reshape(blocks, -1)
    onehot = (
        flattened[:, :, None] == jnp.arange(expert_count, dtype=jnp.int32)[None, None, :]
    ).astype(jnp.int32)
    before = jnp.cumsum(onehot, axis=1) - onehot
    position = jnp.sum(before * onehot, axis=2)
    return flattened * capacity + position


def token_picks(slots, top_count, slot_count):
    blocks = slots.shape[0]
    grouped = slots.reshape(blocks, 1, -1, top_count)
    return jnp.any(grouped == jnp.arange(slot_count, dtype=jnp.int32)[None, :, None, None], axis=3)


def routing_column(route_weights, routed_experts):
    as_float = routed_experts.astype(jnp.float32)
    weights_all, experts_all = (
        lax.all_gather(route_weights, "rep", axis=0, tiled=True),
        lax.all_gather(as_float, "rep", axis=0, tiled=True),
    )
    return (weights_all, experts_all.astype(jnp.int32))


def on_device(tokens, routed_experts, route_weights, gate_weight, up_weight, down_weight):
    replicas = lax.axis_size("rep")
    owners = lax.axis_size("exp")
    token_rows, model_width = tokens.shape
    top_count = routed_experts.shape[1]
    local_experts = gate_weight.shape[0]
    expert_count = local_experts * owners
    capacity = max(2, 3 * token_rows * top_count // (2 * expert_count))
    slot_count = expert_count * capacity
    own_slots = slot_table(routed_experts[None], expert_count, capacity)
    column = None
    column_slots = None
    selected = token_picks(own_slots, top_count, slot_count)[0].astype(jnp.bfloat16)
    buffer = jnp.dot(selected, tokens, preferred_element_type=jnp.float32).astype(jnp.bfloat16)
    buffer = buffer.reshape(owners, local_experts, capacity, model_width)
    arrived = lax.all_to_all(buffer, "exp", split_axis=0, concat_axis=2, tiled=True)
    rows_now = lax.all_gather(arrived, "rep", axis=2, tiled=True)[0]
    gate_value = jnp.einsum(
        "emd,efd->emf", rows_now, gate_weight, preferred_element_type=jnp.float32
    )
    up_value = jnp.einsum("emd,efd->emf", rows_now, up_weight, preferred_element_type=jnp.float32)
    hidden = (jax.nn.silu(gate_value) * up_value).astype(jnp.bfloat16)
    outcome = jnp.einsum("emf,efd->emd", hidden, down_weight, preferred_element_type=jnp.float32)
    outcome = lax.optimization_barrier(outcome.astype(jnp.bfloat16))
    outcomes = outcome[None]
    outcomes = outcomes.reshape(local_experts, replicas, owners, capacity, model_width)
    column = routing_column(route_weights, routed_experts)
    column_slots = slot_table(
        column[1].reshape(replicas, token_rows, top_count), expert_count, capacity
    )
    returned = lax.all_to_all(outcomes, "exp", split_axis=2, concat_axis=0, tiled=True)
    returned = returned.reshape(expert_count, replicas, capacity, model_width)
    expert_index = column_slots // capacity
    place_index = column_slots % capacity
    replica_index = jnp.broadcast_to(
        jnp.arange(replicas, dtype=jnp.int32)[:, None], column_slots.shape
    )
    picked = returned[expert_index, replica_index, place_index].astype(jnp.float32)
    column_weights = column[0].reshape(replicas, token_rows, top_count)
    weighted = jnp.sum(
        picked.reshape(replicas, token_rows, top_count, model_width)
        * column_weights[:, :, :, None],
        axis=2,
    )
    summed = lax.psum_scatter(weighted, "rep", scatter_dimension=0, tiled=True)
    return summed.reshape(token_rows, model_width).astype(jnp.bfloat16)


def solution(mesh):
    placed = (
        P(("rep", "exp"), None),
        P(("rep", "exp"), None),
        P(("rep", "exp"), None),
        P("exp", "rep", None),
        P("exp", "rep", None),
        P("exp", "rep", None),
    )
    return jax.shard_map(
        on_device, mesh=mesh, in_specs=placed, out_specs=P(("rep", "exp"), None), check_vma=False
    )
```

profile of v0, /device:TPU:2, one launch (start us, length us, event | category | flops | bytes accessed | tf_op | source)
XLA Modules:
  0.0 557.9 jit_solution(14770991850050571050)
XLA Ops:
  6.5 0.9 copy.34
  7.4 0.1 eq.65
  7.5 0.1 fusion.25
  7.6 0.2 reduce_window_sum.22
  7.8 0.2 select_reduce_fusion.1
  8.0 0.1 reduce_sum.32
  8.1 0.1 fusion.24
  8.2 2.7 convolution_convert_fusion.1
  10.9 4.1 reshape.225
  15.0 3.6 copy.36
  18.6 28.4 %all_to_all.33 = bf16[32,2,3,4096]{3,1,2,0:T(2,128)(2,1)S(1)} all-to-all(bf16[32,2,3,4096]{3,1,2,0:T(2,128)(2,1)S(1)} %copy.36), channel_id=1, replica_groups=mesh['rep'=8,'exp'=32] {'exp'}, dimensions={0} | all-to-all | bytes 3145728 | tf_op jit(solution)/shard_map/all_to_all | solution.py:48
  47.0 2.1 copy.37
  49.1 134.3 %all-gather.4.cloned.1.call-done = bf16[1,2,768,4096]{3,2,1,0:T(8,128)(2,1)} async-done(((bf16[1,2,96,4096]{3,2,1,0:T(8,128)(2,1)}), bf16[1,2,768,4096]{3,2,1,0:T(8,128)(2,1)}) %all-gather.4.cloned.1.call-update) | async-done | bytes 12582928 | tf_op jit(solution)/shard_map/all_gather | solution.py:49
  183.4 10.9 %fusion.3 = f32[2,768,192]{1,2,0:T(8,128)} fusion(bf16[2,192,4096]{2,1,0:T(8,128)(2,1)} %param.9, bf16[1,2,768,4096]{3,2,1,0:T(8,128)(2,1)} %all-gather.4.cloned.1.call-done), kind=kOutput, calls=%fused_computation.5 | convolution fusion | flops 2415919104 | bytes 16908288 | tf_op jit(solution)/shard_map/emd,efd->emf/dot_general | solution.py:50
  194.3 15.9 %convolution_convert_fusion = bf16[2,768,4096]{2,1,0:T(8,128)(2,1)} fusion(bf16[2,192,4096]{2,1,0:T(8,128)(2,1)S(1)} %copy-done, bf16[2,192,4096]{2,1,0:T(8,128)(2,1)} %param.10, bf16[1,2,768,4096]{3,2,1,0:T(8,128)(2,1)} %all-gather.4.cloned.1.call-done, f32[2,768,192]{1,2,0:T(8,128)} %fusion.3), kind=kOutput, calls=%fused_computation.7 | convolution fusion | flops 4839899136 | bytes 32636928 | tf_op jit(solution)/shard_map/emf,efd->emd/dot_general | solution.py:55
  210.2 21.2 %copy.38 = bf16[2,768,4096]{2,0,1:T(2,128)(2,1)S(1)} copy(bf16[2,768,4096]{2,1,0:T(8,128)(2,1)} %convolution_convert_fusion) | data formatting | bytes 25165824 | tf_op jit(solution)/shard_map/optimization_barrier | solution.py:56
  231.5 11.5 %copy.39 = bf16[2,8,32,3,4096]{4,0,3,1,2:T(2,128)(2,1)} copy(bf16[2,8,32,3,4096]{4,0,3,2,1:T(2,128)(2,1)S(1)} %bitcast.42) | data formatting | bytes 25165824 | tf_op jit(solution)/shard_map/reshape;broadcast_in_dim | solution.py:58
  243.0 7.6 %all-to-all-start.1 = ((bf16[2,8,32,3,4096]{4,0,3,1,2:T(2,128)(2,1)}), bf16[2,8,32,3,4096]{4,0,3,1,2:T(2,128)(2,1)}, u32[]{:S(2)}, u32[]{:S(2)}) async-start(bf16[2,8,32,3,4096]{4,0,3,1,2:T(2,128)(2,1)} %copy.39), calls=%async_computation.1 | async-start | bytes 25165824 | tf_op jit(solution)/shard_map/all_to_all | solution.py:63
  250.6 0.0 reduce-scatter.2.cloned.1.call-start
  250.7 24.9 %all-gather = f32[8,16,8]{1,2,0:T(8,128)S(1)} all-gather(f32[1,16,8]{1,2,0:T(8,128)S(1)} %convert_bitcast_fusion.1), channel_id=1, replica_groups=mesh['rep'=8,'exp'=32] {'rep'}, dimensions={0}, use_global_device_ids=true | all-gather | bytes 4608 | tf_op jit(solution)/shard_map/all_gather | solution.py:28
  275.6 0.1 copy.46
  275.7 2.5 select_reduce_fusion
  278.3 0.1 copy.41
  278.4 0.1 mul.56
  278.5 24.7 %all-gather.1 = f32[8,16,8]{1,2,0:T(8,128)S(1)} all-gather(f32[1,16,8]{1,2,0:T(8,128)S(1)} %bitcast.45), channel_id=1, replica_groups=mesh['rep'=8,'exp'=32] {'rep'}, dimensions={0}, use_global_device_ids=true | all-gather | bytes 4608 | tf_op jit(solution)/shard_map/all_gather | solution.py:27
  303.1 0.1 copy.45
  303.3 115.4 %all-to-all-done.1 = bf16[2,8,32,3,4096]{4,0,3,1,2:T(2,128)(2,1)} async-done(((bf16[2,8,32,3,4096]{4,0,3,1,2:T(2,128)(2,1)}), bf16[2,8,32,3,4096]{4,0,3,1,2:T(2,128)(2,1)}, u32[]{:S(2)}, u32[]{:S(2)}) %all-to-all-start.1) | async-done | bytes 12582944 | tf_op jit(solution)/shard_map/all_to_all | solution.py:63
  418.7 14.5 %copy.40 = bf16[32,2,8,1,3,4096]{5,2,4,1,0,3:T(8,128)(2,1)} copy(bf16[32,2,8,1,3,4096]{5,1,4,2,0,3:T(2,128)(2,1)} %bitcast.6) | data formatting | bytes 25165824 | tf_op jit(solution)/shard_map/all_to_all | solution.py:63
  433.2 34.4 %gather_fusion = bf16[1024,4096]{1,0:T(8,128)(2,1)} fusion(bf16[64,8,3,4096]{3,1,2,0:T(8,128)(2,1)} %bitcast.41, s32[1024]{0:T(1024)S(1)} %fusion.30), kind=kCustom, calls=%fused_computation | custom fusion | bytes 16789504 | tf_op jit(solution)/shard_map/gather | solution.py:70
  467.6 12.9 %fusion = f32[8,16,4096]{2,1,0:T(8,128)} fusion(f32[8,16,8]{2,1,0:T(8,128)S(1)} %copy.45, bf16[1024,4096]{1,0:T(8,128)(2,1)} %gather_fusion), kind=kLoop, calls=%fused_computation.2 | loop fusion | flops 12058624 | bytes 10489856 | tf_op jit(solution)/shard_map/reduce_sum | solution.py:72
  480.6 68.8 %reduce-scatter.2.cloned.1.call-done = f32[1,16,4096]{2,1,0:T(8,128)} async-done(((f32[8,16,4096]{2,1,0:T(8,128)}), f32[1,16,4096]{2,1,0:T(8,128)}) %reduce-scatter.2.cloned.1.call-update) | async-done | bytes 262160 | tf_op jit(solution)/shard_map/reduce_scatter | solution.py:77
  549.4 1.6 convert_bitcast_fusion
  (17 shorter events, 0.2 us)
Async XLA Ops:
  6.5 187.8 %copy-start = (bf16[2,192,4096]{2,1,0:T(8,128)(2,1)S(1)}, bf16[2,192,4096]{2,1,0:T(8,128)(2,1)}, u32[]{:S(2)}) copy-start(bf16[2,192,4096]{2,1,0:T(8,128)(2,1)} %param.11) | copy-start | bytes 9437188
  6.5 176.9 %all-gather.4.cloned.1.call-start = ((), (), s32[]{:S(2)}) async-start(), calls=%async_computation.3 | async-start | bytes 14155776 | tf_op jit(solution)/shard_map/all_gather | solution.py:49
  243.0 7.7 %copy-start.2 = (s32[16,8]{0,1:T(8,128)S(1)}, s32[16,8]{0,1:T(8,128)}, u32[]{:S(2)}) copy-start(s32[16,8]{0,1:T(8,128)} %param.7) | copy-start | bytes 1540
  243.0 35.5 %copy-start.3 = (f32[16,8]{0,1:T(8,128)S(1)}, f32[16,8]{0,1:T(8,128)}, u32[]{:S(2)}) copy-start(f32[16,8]{0,1:T(8,128)} %param.8) | copy-start | bytes 1540
  243.0 175.7 %all-to-all-start.1 = ((bf16[2,8,32,3,4096]{4,0,3,1,2:T(2,128)(2,1)}), bf16[2,8,32,3,4096]{4,0,3,1,2:T(2,128)(2,1)}, u32[]{:S(2)}, u32[]{:S(2)}) async-start(bf16[2,8,32,3,4096]{4,0,3,1,2:T(2,128)(2,1)} %copy.39), calls=%async_computation.1 | async-start | bytes 25165824 | tf_op jit(solution)/shard_map/all_to_all | solution.py:63
  250.6 298.8 %reduce-scatter.2.cloned.1.call-start = ((), (), s32[]{:S(2)}) async-start(), calls=%async_computation.4 | async-start | bytes 2359296 | tf_op jit(solution)/shard_map/reduce_scatter | solution.py:77
  467.6 83.4 %copy-start.1 = (bf16[2,192,4096]{2,1,0:T(8,128)(2,1)S(1)}, bf16[2,192,4096]{2,1,0:T(8,128)(2,1)}, u32[]{:S(2)}) copy-start(bf16[2,192,4096]{2,1,0:T(8,128)(2,1)} %param.11) | copy-start | bytes 9437188
Sparse Core Ops, SparseCore 0:
  49.3 134.1 all-gather.3
  480.7 68.6 reduce-scatter.1
where the time goes:
time: 559 us; the launch traced here: 558 us
  waiting for transfers between devices  319 us (57%)
  local copies, waits for them, and re-layouts  93 us (17%)
  blocking collectives  78 us (14%)
  matrix products  29.5 us (5%)
  other arithmetic  17.7 us (3%)
  between operations  13.5 us (2%)
  starting transfers between devices  7.64 us (1%)
    all_gather x1, waiting for transfers between devices, on_device(): rows_now = lax.all_gather(arrived, 'rep', axis=2, tiled=True)[0]  134 us
    all_to_all x1, waiting for transfers between devices, on_device(): lax.all_to_all(outcomes, 'exp', split_axis=2, concat_axis=0, tiled=True)  115 us
    reduce_scatter x1, waiting for transfers between devices, on_device(): summed = lax.psum_scatter(weighted, 'rep', scatter_dimension=0, tiled=True)  68.8 us
    gather x1, local copies, waits for them, and re-layouts, on_device(): returned[expert_index, replica_index, place_index].astype(jnp.float32)  34.4 us
    all_to_all x1, blocking collectives, on_device(): lax.all_to_all(buffer, 'exp', split_axis=0, concat_axis=2, tiled=True)  28.4 us
    all_gather x1, blocking collectives, routing_column(): lax.all_gather(as_float, 'rep', axis=0, tiled=True)  24.9 us
    all_gather x1, blocking collectives, routing_column(): lax.all_gather(route_weights, 'rep', axis=0, tiled=True)  24.7 us
    optimization_barrier x1, local copies, waits for them, and re-layouts, on_device(): outcome = lax.optimization_barrier(outcome.astype(jnp.bfloat16))  21.2 us
  transfers between devices with their start and end apart: 3, of which 3 were waited for; matrix products, arithmetic and copies ran while one was open for 1% of the time, Pallas kernels for 0%

commit v1 on v0

--- a/solution.py
+++ b/solution.py
@@ -46,7 +46,9 @@
     buffer = jnp.dot(selected, tokens, preferred_element_type=jnp.float32).astype(jnp.bfloat16)
     buffer = buffer.reshape(owners, local_experts, capacity, model_width)
     arrived = lax.all_to_all(buffer, "exp", split_axis=0, concat_axis=2, tiled=True)
-    rows_now = lax.all_gather(arrived, "rep", axis=2, tiled=True)[0]
+    rows_now = jnp.concatenate(
+        lax.all_to_all(jnp.stack(lax.axis_size("rep") * [arrived], axis=0), "rep", 0, 0), axis=2
+    )[0]
     gate_value = jnp.einsum(
         "emd,efd->emf", rows_now, gate_weight, preferred_element_type=jnp.float32
     )

time: 559 us -> 719 us (1.29)
  blocking collectives: 78 us -> 363 us
  waiting for transfers between devices: 319 us -> 182 us
  local copies, waits for them, and re-layouts: 93 us -> 106 us
    all_to_all x0 -> x1, blocking collectives: none -> 285 us  [on_device(): lax.all_to_all(jnp.stack(lax.axis_size('rep') * [arrived], axis=0), 'rep'...]
    all_gather x1 -> x0, waiting for transfers between devices: 134 us -> none  [on_device(): rows_now = lax.all_gather(arrived, 'rep', axis=2, tiled=True)[0]]
    another operation x0 -> x2, local copies, waits for them, and re-layouts: none -> 9.64 us  [on_device(): jnp.stack(lax.axis_size('rep') * [arrived], axis=0)]
  transfers between devices with their start and end apart: 3 -> 2, of which waited for: 3 -> 2; matrix products, arithmetic and copies ran while one was open for 1% -> 0% of each run, Pallas kernels for 0% -> 0%
where the time goes in v1:
time: 719 us; the launch traced here: 718 us
  blocking collectives  363 us (50%)
  waiting for transfers between devices  182 us (25%)
  local copies, waits for them, and re-layouts  106 us (15%)
  matrix products  29.5 us (4%)
  other arithmetic  17.7 us (2%)
  between operations  13.5 us (2%)
    all_to_all x1, blocking collectives, on_device(): lax.all_to_all(jnp.stack(lax.axis_size('rep') * [arrived], axis=0), 'rep'...  285 us
    all_to_all x1, waiting for transfers between devices, on_device(): lax.all_to_all(outcomes, 'exp', split_axis=2, concat_axis=0, tiled=True)  114 us
    reduce_scatter x1, waiting for transfers between devices, on_device(): summed = lax.psum_scatter(weighted, 'rep', scatter_dimension=0, tiled=True)  68 us
    gather x1, local copies, waits for them, and re-layouts, on_device(): returned[expert_index, replica_index, place_index].astype(jnp.float32)  34.4 us
    all_to_all x1, blocking collectives, on_device(): lax.all_to_all(buffer, 'exp', split_axis=0, concat_axis=2, tiled=True)  28.4 us
    all_gather x1, blocking collectives, routing_column(): lax.all_gather(route_weights, 'rep', axis=0, tiled=True)  24.9 us
    all_gather x1, blocking collectives, routing_column(): lax.all_gather(as_float, 'rep', axis=0, tiled=True)  24.7 us
    optimization_barrier x1, local copies, waits for them, and re-layouts, on_device(): outcome = lax.optimization_barrier(outcome.astype(jnp.bfloat16))  21.2 us
  transfers between devices with their start and end apart: 2, of which 2 were waited for; matrix products, arithmetic and copies ran while one was open for 0% of the time, Pallas kernels for 0%

profile of v1, /device:TPU:2, one launch (start us, length us, event | category | flops | bytes accessed | tf_op | source)
XLA Modules:
  0.0 718.3 jit_solution(1712563968607605538)
XLA Ops:
  6.5 0.9 copy.34
  7.4 0.1 eq.65
  7.5 0.1 fusion.14
  7.6 0.2 reduce_window_sum.22
  7.8 0.2 select_reduce_fusion.1
  8.0 0.1 reduce_sum.32
  8.1 0.1 fusion.13
  8.2 2.7 convolution_convert_fusion.1
  10.9 4.1 reshape.233
  15.0 3.6 copy.36
  18.6 28.4 %all_to_all.35 = bf16[32,2,3,4096]{3,1,2,0:T(2,128)(2,1)S(1)} all-to-all(bf16[32,2,3,4096]{3,1,2,0:T(2,128)(2,1)S(1)} %copy.36), channel_id=1, replica_groups=mesh['rep'=8,'exp'=32] {'exp'}, dimensions={0} | all-to-all | bytes 3145728 | tf_op jit(solution)/shard_map/all_to_all | solution.py:48
  47.0 2.1 copy.37
  49.1 7.6 %stack.5 = bf16[8,1,2,96,4096]{4,3,2,1,0:T(8,128)(2,1)} broadcast(bf16[2,96,4096]{2,1,0:T(8,128)(2,1)} %copy.37), dimensions={2,3,4} | broadcast | bytes 14155776 | tf_op jit(solution)/shard_map/stack | solution.py:50
  56.7 285.3 %all_to_all.36 = bf16[8,1,2,96,4096]{4,3,2,1,0:T(8,128)(2,1)S(1)} all-to-all(bf16[8,1,2,96,4096]{4,3,2,1,0:T(8,128)(2,1)} %stack.5), channel_id=1, replica_groups=mesh['rep'=8,'exp'=32] {'rep'}, dimensions={0} | all-to-all | bytes 25165824 | tf_op jit(solution)/shard_map/all_to_all | solution.py:50
  341.9 5.1 copy.38
  347.1 10.8 %fusion.24 = f32[2,768,192]{1,2,0:T(8,128)} fusion(bf16[2,768,4096]{2,1,0:T(8,128)(2,1)} %bitcast.37, bf16[2,192,4096]{2,1,0:T(8,128)(2,1)} %param.9), kind=kOutput, calls=%fused_computation.44 | convolution fusion | flops 2415919104 | bytes 16908288 | tf_op jit(solution)/shard_map/emd,efd->emf/dot_general | solution.py:52
  357.9 15.9 %convolution_convert_fusion = bf16[2,768,4096]{2,1,0:T(8,128)(2,1)} fusion(bf16[2,192,4096]{2,1,0:T(8,128)(2,1)S(1)} %copy-done, bf16[2,768,4096]{2,1,0:T(8,128)(2,1)} %bitcast.38, bf16[2,192,4096]{2,1,0:T(8,128)(2,1)} %param.10, f32[2,768,192]{1,2,0:T(8,128)} %fusion.24), kind=kOutput, calls=%fused_computation.3 | convolution fusion | flops 4839899136 | bytes 32636928 | tf_op jit(solution)/shard_map/emf,efd->emd/dot_general | solution.py:57
  373.8 21.2 %copy.39 = bf16[2,768,4096]{2,0,1:T(2,128)(2,1)S(1)} copy(bf16[2,768,4096]{2,1,0:T(8,128)(2,1)} %convolution_convert_fusion) | data formatting | bytes 25165824 | tf_op jit(solution)/shard_map/optimization_barrier | solution.py:58
  395.1 11.5 %copy.40 = bf16[2,8,32,3,4096]{4,0,3,1,2:T(2,128)(2,1)} copy(bf16[2,8,32,3,4096]{4,0,3,2,1:T(2,128)(2,1)S(1)} %bitcast.36) | data formatting | bytes 25165824 | tf_op jit(solution)/shard_map/reshape;broadcast_in_dim | solution.py:60
  406.6 6.4 all-to-all-start.2
  413.1 24.7 %all-gather = f32[8,16,8]{1,2,0:T(8,128)S(1)} all-gather(f32[1,16,8]{1,2,0:T(8,128)S(1)} %convert_bitcast_fusion.1), channel_id=1, replica_groups=mesh['rep'=8,'exp'=32] {'rep'}, dimensions={0}, use_global_device_ids=true | all-gather | bytes 4608 | tf_op jit(solution)/shard_map/all_gather | solution.py:28
  437.8 0.1 copy.47
  437.9 2.5 select_reduce_fusion
  440.4 0.1 copy.42
  440.5 0.1 mul.56
  440.7 24.9 %all-gather.1 = f32[8,16,8]{1,2,0:T(8,128)S(1)} all-gather(f32[1,16,8]{1,2,0:T(8,128)S(1)} %bitcast.41), channel_id=1, replica_groups=mesh['rep'=8,'exp'=32] {'rep'}, dimensions={0}, use_global_device_ids=true | all-gather | bytes 4608 | tf_op jit(solution)/shard_map/all_gather | solution.py:27
  465.7 114.3 %all-to-all-done.2 = bf16[2,8,32,3,4096]{4,0,3,1,2:T(2,128)(2,1)} async-done(((bf16[2,8,32,3,4096]{4,0,3,1,2:T(2,128)(2,1)}), bf16[2,8,32,3,4096]{4,0,3,1,2:T(2,128)(2,1)}, u32[]{:S(2)}, u32[]{:S(2)}) %all-to-all-start.2) | async-done | bytes 12582944 | tf_op jit(solution)/shard_map/all_to_all | solution.py:65
  579.9 14.5 %copy.41 = bf16[32,2,8,1,3,4096]{5,2,4,1,0,3:T(8,128)(2,1)} copy(bf16[32,2,8,1,3,4096]{5,1,4,2,0,3:T(2,128)(2,1)} %bitcast.7) | data formatting | bytes 25165824 | tf_op jit(solution)/shard_map/all_to_all | solution.py:65
  594.4 34.4 %gather_fusion = bf16[1024,4096]{1,0:T(8,128)(2,1)} fusion(bf16[64,8,3,4096]{3,1,2,0:T(8,128)(2,1)} %bitcast.34, s32[1024]{0:T(1024)S(1)} %fusion.19), kind=kCustom, calls=%fused_computation | custom fusion | bytes 16789504 | tf_op jit(solution)/shard_map/gather | solution.py:72
  628.9 12.9 %fusion = f32[8,16,4096]{2,1,0:T(8,128)} fusion(f32[8,16,8]{2,1,0:T(8,128)S(1)} %copy.46, bf16[1024,4096]{1,0:T(8,128)(2,1)} %gather_fusion), kind=kLoop, calls=%fused_computation.2 | loop fusion | flops 12058624 | bytes 10489856 | tf_op jit(solution)/shard_map/reduce_sum | solution.py:74
  641.8 68.0 %reduce-scatter.2.cloned.1.call-done = f32[1,16,4096]{2,1,0:T(8,128)} async-done(((f32[8,16,4096]{2,1,0:T(8,128)}), f32[1,16,4096]{2,1,0:T(8,128)}) %reduce-scatter.2.cloned.1.call-update) | async-done | bytes 262160 | tf_op jit(solution)/shard_map/reduce_scatter | solution.py:79
  709.8 1.6 convert_bitcast_fusion
  (17 shorter events, 0.2 us)
Async XLA Ops:
  6.5 351.4 %copy-start = (bf16[2,192,4096]{2,1,0:T(8,128)(2,1)S(1)}, bf16[2,192,4096]{2,1,0:T(8,128)(2,1)}, u32[]{:S(2)}) copy-start(bf16[2,192,4096]{2,1,0:T(8,128)(2,1)} %param.11) | copy-start | bytes 9437188
  406.6 6.5 copy-start.2
  406.6 34.0 %copy-start.3 = (f32[16,8]{0,1:T(8,128)S(1)}, f32[16,8]{0,1:T(8,128)}, u32[]{:S(2)}) copy-start(f32[16,8]{0,1:T(8,128)} %param.8) | copy-start | bytes 1540
  406.6 173.3 %all-to-all-start.2 = ((bf16[2,8,32,3,4096]{4,0,3,1,2:T(2,128)(2,1)}), bf16[2,8,32,3,4096]{4,0,3,1,2:T(2,128)(2,1)}, u32[]{:S(2)}, u32[]{:S(2)}) async-start(bf16[2,8,32,3,4096]{4,0,3,1,2:T(2,128)(2,1)} %copy.40), calls=%async_computation.2 | async-start | bytes 25165824 | tf_op jit(solution)/shard_map/all_to_all | solution.py:65
  413.0 296.8 %reduce-scatter.2.cloned.1.call-start = ((), (), s32[]{:S(2)}) async-start(), calls=%async_computation.4 | async-start | bytes 2359296 | tf_op jit(solution)/shard_map/reduce_scatter | solution.py:79
  628.9 82.6 %copy-start.1 = (bf16[2,192,4096]{2,1,0:T(8,128)(2,1)S(1)}, bf16[2,192,4096]{2,1,0:T(8,128)(2,1)}, u32[]{:S(2)}) copy-start(bf16[2,192,4096]{2,1,0:T(8,128)(2,1)} %param.11) | copy-start | bytes 9437188
Sparse Core Ops, SparseCore 0:
  641.9 67.7 reduce-scatter.1
